TPU v7x, 32 devices: a whole 2x2x4 slice. The times are simulated.
32 devices in a mesh: fsdp: 4 (over z), ctx: 2 (over x), tp: 4 (over y, core).
Axes of the slice: x: 2, y: 2, z: 4, core: 2. Of those that a mesh axis runs over, the one named last changes fastest.
Arguments:
- tokens: bfloat16 [4, 2048, 2048], P('fsdp', 'ctx'), may hold values from -6 to 6
- segments: int32 [4, 2048], P('fsdp'), may hold values from 0 to 7, never falling along the last dimension, each value on 1 to 1024 neighbouring positions
- cotangent: bfloat16 [4, 2048, 2048], P('fsdp', 'ctx'), may hold values from -6 to 6
- gain_mix: float32 [2048], replicated, may hold values from 0.5 to 1.5
- w_branch: bfloat16 [2048, 2560], P('fsdp', 'tp'), may hold values from -0.125 to 0.125
- w_input: bfloat16 [2048, 2560], P('fsdp', 'tp'), may hold values from -0.125 to 0.125
- conv_weight: float32 [4, 2560], P(None, 'tp'), may hold values from -3 to 3
- conv_bias: float32 [2560], P('tp'), may hold values from -1.75 to 1.75
- gate_a: bfloat16 [16, 160, 160], P('tp'), may hold values from -0.5 to 0.5
- bias_a: float32 [2560], P('tp'), may hold values from -3 to 3
- gate_x: bfloat16 [16, 160, 160], P('tp'), may hold values from -0.5 to 0.5
- bias_x: float32 [2560], P('tp'), may hold values from -3 to 3
- decay_param: float32 [2560], P('tp'), may hold values from 4 to 8
- w_out: bfloat16 [2560, 2048], P('tp', 'fsdp'), may hold values from -0.3125 to 0.3125
- gain_mlp: float32 [2048], replicated, may hold values from 0.5 to 1.5
- w_gate: bfloat16 [2048, 6144], P('fsdp', 'tp'), may hold values from -0.125 to 0.125
- w_up: bfloat16 [2048, 6144], P('fsdp', 'tp'), may hold values from -0.125 to 0.125
- w_down: bfloat16 [6144, 2048], P('tp', 'fsdp'), may hold values from -0.15625 to 0.15625
Outputs:
- output: bfloat16 [4, 2048, 2048], P('fsdp', 'ctx')
- grad_tokens: bfloat16 [4, 2048, 2048], P('fsdp', 'ctx')
- grad_gain_mix: float32 [2048], replicated
- grad_w_branch: float32 [2048, 2560], P('fsdp', 'tp')
- grad_w_input: float32 [2048, 2560], P('fsdp', 'tp')
- grad_conv_weight: float32 [4, 2560], P(None, 'tp')
- grad_conv_bias: float32 [2560], P('tp')
- grad_gate_a: float32 [16, 160, 160], P('tp')
- grad_bias_a: float32 [2560], P('tp')
- grad_gate_x: float32 [16, 160, 160], P('tp')
- grad_bias_x: float32 [2560], P('tp')
- grad_decay_param: float32 [2560], P('tp')
- grad_w_out: float32 [2560, 2048], P('tp', 'fsdp')
- grad_gain_mlp: float32 [2048], replicated
- grad_w_gate: float32 [2048, 6144], P('fsdp', 'tp')
- grad_w_up: float32 [2048, 6144], P('fsdp', 'tp')
- grad_w_down: float32 [6144, 2048], P('tp', 'fsdp')
Inputs may be any that keep to these rules, and one draw needn't show every extreme that they name: `segments`: within a sequence the document numbers never fall; every document has 1 to 1024 positions and one has exactly 1024.
All inputs are finite; a program needn't handle non-finite values.
Results may differ from a plain program's by a relative error of at most 0.012.
Values may be sent and summed in bfloat16 or wider, within the bound.
A program may use at most 256 MiB of HBM per device.

v0:
```python
import jax
import jax.numpy as jnp
from jax import lax
from jax.sharding import PartitionSpec as P

EPSILON = 1e-06
RATE_SCALE = 8.0


def passed_along(block, axis, distance):
    devices = range(lax.axis_size(axis))
    route = [(i - distance, i) for i in devices if i - distance in devices]
    return lax.ppermute(block, axis, route)


def entering_2(x, axis, combine, identity, reverse):
    length, place = (lax.axis_size(axis), lax.axis_index(axis))
    everything = jax.tree.map(lambda part: lax.all_gather(part, axis), x)
    start = jax.tree.map(
        lambda part, zero: jnp.broadcast_to(jnp.asarray(zero, part.dtype), part.shape), x, identity
    )

    def turn(k, before):
        at = length - 1 - k if reverse else k
        reached = at > place if reverse else at < place
        new = combine(before, jax.tree.map(lambda part: part[at], everything))
        return jax.tree.map(lambda a, b: jnp.where(reached, a, b), new, before)

    return lax.fori_loop(0, length, turn, start)


def linear_combine(earlier, later):
    return (earlier[0] * later[0], later[0] * earlier[1] + later[1])


def matmul(left, right):
    return jnp.dot(left, right, preferred_element_type=jnp.float32)


def left_inner(left, right):
    return lax.dot_general(
        left, right, (((0,), (0,)), ((), ())), preferred_element_type=jnp.float32
    )


def right_inner(left, right):
    return lax.dot_general(
        left, right, (((1,), (1,)), ((), ())), preferred_element_type=jnp.float32
    )


def gelu_slope(values):
    result, pull_back = jax.vjp(lambda inner_v: jax.nn.gelu(inner_v, approximate=True), values)
    return (result, pull_back(jnp.ones_like(values))[0])


def rms_rows(values):
    return lax.rsqrt(jnp.mean(values * values, axis=-1, keepdims=True) + EPSILON)


def norm_back(grad_norm, scaled, scale_row, gain):
    grad_scaled = grad_norm * gain
    return scale_row * (
        grad_scaled - scaled * jnp.mean(grad_scaled * scaled, axis=-1, keepdims=True)
    )


def shards(
    tokens,
    segments,
    cotangent,
    gain_mix,
    w_branch,
    w_input,
    conv_weight,
    conv_bias,
    gate_a,
    bias_a,
    gate_x,
    bias_x,
    decay_param,
    w_out,
    gain_mlp,
    w_gate,
    w_up,
    w_down,
):
    full_branch, full_input, full_gate, full_up, full_out, full_down = (
        lax.all_gather(w_branch, "fsdp", axis=0, tiled=True),
        lax.all_gather(w_input, "fsdp", axis=0, tiled=True),
        lax.all_gather(w_gate, "fsdp", axis=0, tiled=True),
        lax.all_gather(w_up, "fsdp", axis=0, tiled=True),
        lax.all_gather(w_out, "fsdp", axis=1, tiled=True),
        lax.all_gather(w_down, "fsdp", axis=1, tiled=True),
    )
    seq_count, tok_count, model_width = tokens.shape
    row_count = seq_count * tok_count
    kernel = conv_weight.shape[0]
    lag_rows = kernel - 1
    local_width = conv_bias.shape[0]
    head_count = gate_a.shape[0]
    block_width = gate_a.shape[1]
    inputs = tokens.reshape(row_count, model_width).astype(jnp.float32)
    scale_mix = rms_rows(inputs)
    scaled_mix = inputs * scale_mix
    normed = (scaled_mix * gain_mix).astype(jnp.bfloat16)
    branch_pre = matmul(normed, full_branch)
    branch, branch_slope = gelu_slope(branch_pre)
    conv_in = (
        matmul(normed, full_input).astype(jnp.bfloat16).reshape(seq_count, tok_count, local_width)
    )
    first_pos = lax.axis_index("ctx") * tok_count
    padded_seg = jnp.pad(segments, ((0, 0), (lag_rows, lag_rows)), constant_values=-1)
    near_seg = lax.dynamic_slice_in_dim(padded_seg, first_pos, tok_count + 2 * lag_rows, 1)
    own_seg = near_seg[:, lag_rows : lag_rows + tok_count]
    same_back = [
        near_seg[:, lag_rows - offset : lag_rows - offset + tok_count] == own_seg
        for offset in range(kernel)
    ]
    same_ahead = [
        near_seg[:, lag_rows + offset : lag_rows + offset + tok_count] == own_seg
        for offset in range(kernel)
    ]
    tail_rows = passed_along(conv_in[:, tok_count - lag_rows :], "ctx", 1)
    conv_ext = jnp.concatenate([tail_rows, conv_in], axis=1)
    conv_sum = jnp.zeros((seq_count, tok_count, local_width), jnp.float32) + conv_bias
    for offset in range(kernel):
        earlier_in = jnp.where(
            same_back[offset][..., None],
            conv_ext[:, lag_rows - offset : lag_rows - offset + tok_count],
            0.0,
        )
        conv_sum = conv_sum + conv_weight[offset] * earlier_in
    conv_out = conv_sum.astype(jnp.bfloat16)
    conv_heads = conv_out.reshape(seq_count, tok_count, head_count, block_width)
    pre_a = (
        jnp.einsum(
            "sthi,hij->sthj", conv_heads, gate_a, preferred_element_type=jnp.float32
        ).reshape(seq_count, tok_count, local_width)
        + bias_a
    )
    pre_x = (
        jnp.einsum(
            "sthi,hij->sthj", conv_heads, gate_x, preferred_element_type=jnp.float32
        ).reshape(seq_count, tok_count, local_width)
        + bias_x
    )
    recur_gate = jax.nn.sigmoid(pre_a)
    input_gate = jax.nn.sigmoid(pre_x)
    softened = jax.nn.softplus(-decay_param)
    log_decay = -RATE_SCALE * softened * recur_gate
    decay = jnp.exp(log_decay)
    root_term = jnp.sqrt(-jnp.expm1(2.0 * log_decay))
    starts = jnp.logical_not(same_back[1])[..., None]
    multiplier = jnp.where(starts, 1.0, root_term)
    carry_factor = jnp.where(starts, 0.0, decay)
    conv_float = conv_out.astype(jnp.float32)
    driven = input_gate * conv_float * multiplier
    decay_run, local_states = lax.associative_scan(linear_combine, (carry_factor, driven), axis=1)
    ones_state = jnp.ones((seq_count, local_width), jnp.float32)
    zero_state = jnp.zeros((seq_count, local_width), jnp.float32)
    entering = entering_2(
        (decay_run[:, -1], local_states[:, -1]),
        "ctx",
        linear_combine,
        (ones_state, zero_state),
        False,
    )[1]
    states = local_states + decay_run * entering[:, None]
    states_rows = states.reshape(row_count, local_width)
    mixed_out = (states_rows * branch).astype(jnp.bfloat16)
    mixer_term = matmul(mixed_out, full_out)
    resid_rows = inputs + lax.psum(mixer_term, "tp")
    scale_mlp = rms_rows(resid_rows)
    scaled_mlp = resid_rows * scale_mlp
    normed_mlp = (scaled_mlp * gain_mlp).astype(jnp.bfloat16)
    gate_pre = matmul(normed_mlp, full_gate)
    up_pre = matmul(normed_mlp, full_up)
    gate_act, gate_slope = gelu_slope(gate_pre)
    hidden = (gate_act * up_pre).astype(jnp.bfloat16)
    down_term = matmul(hidden, full_down)
    output = (resid_rows + lax.psum(down_term, "tp")).astype(jnp.bfloat16)
    grad_low = cotangent.reshape(row_count, model_width)
    grad_out = grad_low.astype(jnp.float32)
    grad_w_down = left_inner(hidden, grad_low)
    grad_hidden = right_inner(grad_low, full_down)
    grad_gate = (grad_hidden * up_pre * gate_slope).astype(jnp.bfloat16)
    grad_up = (grad_hidden * gate_act).astype(jnp.bfloat16)
    grad_w_gate = left_inner(normed_mlp, grad_gate)
    grad_w_up = left_inner(normed_mlp, grad_up)
    mlp_back_term = right_inner(grad_gate, full_gate) + right_inner(grad_up, full_up)
    grad_norm_mlp = lax.psum(mlp_back_term, "tp")
    grad_resid = grad_out + norm_back(grad_norm_mlp, scaled_mlp, scale_mlp, gain_mlp)
    grad_proj = grad_resid.astype(jnp.bfloat16)
    grad_gain_mlp = jnp.sum(grad_norm_mlp * scaled_mlp, axis=0)
    grad_w_out = left_inner(mixed_out, grad_proj)
    grad_mixed = right_inner(grad_proj, full_out)
    grad_branch = (grad_mixed * states_rows * branch_slope).astype(jnp.bfloat16)
    grad_states = (grad_mixed * branch).reshape(seq_count, tok_count, local_width)
    next_factor = jnp.concatenate(
        [carry_factor[:, 1:], jnp.ones((seq_count, 1, local_width), jnp.float32)], axis=1
    )
    run_back, local_back = lax.associative_scan(
        linear_combine, (jnp.flip(next_factor, 1), jnp.flip(grad_states, 1)), axis=1
    )
    run_back = jnp.flip(run_back, 1)
    local_back = jnp.flip(local_back, 1)
    leaving = (carry_factor[:, 0] * run_back[:, 0], carry_factor[:, 0] * local_back[:, 0])
    arriving = entering_2(leaving, "ctx", linear_combine, (ones_state, zero_state), True)[1]
    grad_total = local_back + run_back * arriving[:, None]
    prev_states = jnp.concatenate([entering[:, None], states[:, :-1]], axis=1)
    grad_mult = grad_total * input_gate * conv_float
    grad_log = jnp.where(
        starts, 0.0, grad_total * prev_states * decay - grad_mult * decay * decay / root_term
    )
    grad_decay_param = (
        RATE_SCALE * jax.nn.sigmoid(-decay_param) * jnp.sum(grad_log * recur_gate, axis=(0, 1))
    )
    grad_pre_a = (grad_log * (-RATE_SCALE * softened) * recur_gate * (1.0 - recur_gate)).astype(
        jnp.bfloat16
    )
    grad_pre_x = (grad_total * conv_float * multiplier * input_gate * (1.0 - input_gate)).astype(
        jnp.bfloat16
    )
    heads_a = grad_pre_a.reshape(seq_count, tok_count, head_count, block_width)
    heads_x = grad_pre_x.reshape(seq_count, tok_count, head_count, block_width)
    grad_gate_a = jnp.einsum(
        "sthi,sthj->hij", conv_heads, heads_a, preferred_element_type=jnp.float32
    )
    grad_gate_x = jnp.einsum(
        "sthi,sthj->hij", conv_heads, heads_x, preferred_element_type=jnp.float32
    )
    grad_bias_a = jnp.sum(grad_pre_a.astype(jnp.float32), axis=(0, 1))
    grad_bias_x = jnp.sum(grad_pre_x.astype(jnp.float32), axis=(0, 1))
    gate_back = jnp.einsum(
        "sthj,hij->sthi", heads_a, gate_a, preferred_element_type=jnp.float32
    ) + jnp.einsum("sthj,hij->sthi", heads_x, gate_x, preferred_element_type=jnp.float32)
    grad_conv = grad_total * input_gate * multiplier + gate_back.reshape(
        seq_count, tok_count, local_width
    )
    head_rows = passed_along(grad_conv[:, :lag_rows], "ctx", -1)
    grad_ext = jnp.concatenate([grad_conv, head_rows], axis=1)
    grad_conv_in = jnp.zeros((seq_count, tok_count, local_width), jnp.float32)
    weight_rows = []
    for offset in range(kernel):
        later_grad = jnp.where(
            same_ahead[offset][..., None], grad_ext[:, offset : offset + tok_count], 0.0
        )
        grad_conv_in = grad_conv_in + conv_weight[offset] * later_grad
        earlier_in = jnp.where(
            same_back[offset][..., None],
            conv_ext[:, lag_rows - offset : lag_rows - offset + tok_count],
            0.0,
        )
        weight_rows.append(jnp.sum(grad_conv * earlier_in, axis=(0, 1)))
    grad_conv_weight = jnp.stack(weight_rows)
    grad_conv_bias = jnp.sum(grad_conv, axis=(0, 1))
    grad_in_low = grad_conv_in.astype(jnp.bfloat16).reshape(row_count, local_width)
    grad_w_input = left_inner(normed, grad_in_low)
    grad_w_branch = left_inner(normed, grad_branch)
    mix_back_term = right_inner(grad_in_low, full_input) + right_inner(grad_branch, full_branch)
    grad_norm_mix = lax.psum(mix_back_term, "tp")
    grad_gain_mix = jnp.sum(grad_norm_mix * scaled_mix, axis=0)
    grad_tokens = (grad_resid + norm_back(grad_norm_mix, scaled_mix, scale_mix, gain_mix)).astype(
        jnp.bfloat16
    )
    owned = (
        lax.psum_scatter(grad_w_branch, "fsdp", scatter_dimension=0, tiled=True),
        lax.psum_scatter(grad_w_input, "fsdp", scatter_dimension=0, tiled=True),
        lax.psum_scatter(grad_w_gate, "fsdp", scatter_dimension=0, tiled=True),
        lax.psum_scatter(grad_w_up, "fsdp", scatter_dimension=0, tiled=True),
        lax.psum_scatter(grad_w_out, "fsdp", scatter_dimension=1, tiled=True),
        lax.psum_scatter(grad_w_down, "fsdp", scatter_dimension=1, tiled=True),
    )
    owned_branch, owned_input, owned_gate, owned_up, owned_out, owned_down = owned
    summed = lax.psum(
        (owned_branch, owned_input, owned_gate, owned_up, owned_out, owned_down), "ctx"
    )
    sum_branch, sum_input, sum_gate, sum_up, sum_out, sum_down = summed
    small_sums = lax.psum(
        (
            grad_gain_mix,
            grad_gain_mlp,
            grad_conv_weight,
            grad_conv_bias,
            grad_gate_a,
            grad_bias_a,
            grad_gate_x,
            grad_bias_x,
            grad_decay_param,
        ),
        ("fsdp", "ctx"),
    )
    (
        sum_gain_mix,
        sum_gain_mlp,
        sum_conv_weight,
        sum_conv_bias,
        sum_gate_a,
        sum_bias_a,
        sum_gate_x,
        sum_bias_x,
        sum_decay,
    ) = small_sums
    return (
        output.reshape(seq_count, tok_count, model_width),
        grad_tokens.reshape(seq_count, tok_count, model_width),
        sum_gain_mix,
        sum_branch,
        sum_input,
        sum_conv_weight,
        sum_conv_bias,
        sum_gate_a,
        sum_bias_a,
        sum_gate_x,
        sum_bias_x,
        sum_decay,
        sum_out,
        sum_gain_mlp,
        sum_gate,
        sum_up,
        sum_down,
    )


def solution(mesh):
    in_specs = (
        P("fsdp", "ctx", None),
        P("fsdp", None),
        P("fsdp", "ctx", None),
        P(),
        P("fsdp", "tp"),
        P("fsdp", "tp"),
        P(None, "tp"),
        P("tp"),
        P("tp", None, None),
        P("tp"),
        P("tp", None, None),
        P("tp"),
        P("tp"),
        P("tp", "fsdp"),
        P(),
        P("fsdp", "tp"),
        P("fsdp", "tp"),
        P("tp", "fsdp"),
    )
    out_specs = (
        P("fsdp", "ctx", None),
        P("fsdp", "ctx", None),
        P(),
        P("fsdp", "tp"),
        P("fsdp", "tp"),
        P(None, "tp"),
        P("tp"),
        P("tp", None, None),
        P("tp"),
        P("tp", None, None),
        P("tp"),
        P("tp"),
        P("tp", "fsdp"),
        P(),
        P("fsdp", "tp"),
        P("fsdp", "tp"),
        P("tp", "fsdp"),
    )
    return jax.shard_map(shards, mesh=mesh, in_specs=in_specs, out_specs=out_specs, check_vma=False)
```

profile of v0, /device:TPU:0, one launch (start us, length us, event | category | flops | bytes accessed | tf_op | source)
XLA Modules:
  0.0 3015.9 jit_solution(510944161602865288)
XLA Ops:
  13.5 53.5 %all-gather.7.cloned.1.call-done = bf16[2048,640]{1,0:T(8,128)(2,1)} async-done(((bf16[512,640]{1,0:T(8,128)(2,1)}), bf16[2048,640]{1,0:T(8,128)(2,1)}) %all-gather.7.cloned.1.call-update) | async-done | bytes 2621456 | tf_op jit(solution)/shard_map/all_gather | solution.py:90
  377.1 12.8 fusion.76
  400.8 150.4 %all-reduce.93.cloned.1.call-done = f32[1024,2048]{1,0:T(8,128)} async-done(((f32[1024,2048]{1,0:T(8,128)}), f32[1024,2048]{1,0:T(8,128)}) %all-reduce.93.cloned.1.call-update) | async-done | bytes 8388624 | tf_op jit(solution)/shard_map/psum | solution.py:173
  563.1 105.0 %all-gather.13.cloned.1.call-done = bf16[2048,1536]{1,0:T(8,128)(2,1)} async-done(((bf16[512,1536]{1,0:T(8,128)(2,1)}), bf16[2048,1536]{1,0:T(8,128)(2,1)}) %all-gather.13.cloned.1.call-update) | async-done | bytes 6291472 | tf_op jit(solution)/shard_map/all_gather | solution.py:91
  668.1 12.2 fusion.139
  680.3 102.8 %all-gather.15.cloned.1.call-done = bf16[2048,1536]{1,0:T(8,128)(2,1)} async-done(((bf16[512,1536]{1,0:T(8,128)(2,1)}), bf16[2048,1536]{1,0:T(8,128)(2,1)}) %all-gather.15.cloned.1.call-update) | async-done | bytes 6291472 | tf_op jit(solution)/shard_map/all_gather | solution.py:92
  794.8 103.4 %all-gather.17.cloned.1.call-done = bf16[1536,2048]{1,0:T(8,128)(2,1)} async-done(((bf16[1536,512]{1,0:T(8,128)(2,1)}), bf16[1536,2048]{1,0:T(8,128)(2,1)}) %all-gather.17.cloned.1.call-update) | async-done | bytes 6291472 | tf_op jit(solution)/shard_map/all_gather | solution.py:94
  898.2 18.2 multiply_convert_fusion.1
  937.2 151.2 %all-reduce.95.cloned.1.call-done = f32[1024,2048]{1,0:T(8,128)} async-done(((f32[1024,2048]{1,0:T(8,128)}), f32[1024,2048]{1,0:T(8,128)}) %all-reduce.95.cloned.1.call-update) | async-done | bytes 8388624 | tf_op jit(solution)/shard_map/psum | solution.py:192
  1166.0 12.5 fusion.54
  1178.4 20.8 reverse.9
  1478.5 20.8 rev.13
  1499.3 20.9 rev.12
  1568.8 12.6 fusion.145
  1581.6 12.5 fusion.146
  1594.1 12.2 fusion.30
  1632.6 29.5 reduce-scatter.9.cloned.1.call-done
  1662.1 214.6 %reduce-scatter.13.cloned.1.call-done = f32[512,1536]{1,0:T(8,128)} async-done(((f32[2048,1536]{1,0:T(8,128)}), f32[512,1536]{1,0:T(8,128)}) %reduce-scatter.13.cloned.1.call-update) | async-done | bytes 3145744 | tf_op jit(solution)/shard_map/reduce_scatter | solution.py:270
  1876.7 215.3 %reduce-scatter.15.cloned.1.call-done = f32[512,1536]{1,0:T(8,128)} async-done(((f32[2048,1536]{1,0:T(8,128)}), f32[512,1536]{1,0:T(8,128)}) %reduce-scatter.15.cloned.1.call-update) | async-done | bytes 3145744 | tf_op jit(solution)/shard_map/reduce_scatter | solution.py:271
  2092.0 215.2 %reduce-scatter.17.cloned.1.call-done = f32[1536,512]{1,0:T(8,128)} async-done(((f32[1536,2048]{1,0:T(8,128)}), f32[1536,512]{1,0:T(8,128)}) %reduce-scatter.17.cloned.1.call-update) | async-done | bytes 3145744 | tf_op jit(solution)/shard_map/reduce_scatter | solution.py:273
  2307.9 291.2 %all-reduce.99.cloned.1.call-done = (f32[1024,2048]{1,0:T(8,128)}, f32[1024,2048]{1,0:T(8,128)}) async-done(((f32[1024,2048]{1,0:T(8,128)}, f32[1024,2048]{1,0:T(8,128)}), (f32[1024,2048]{1,0:T(8,128)}, f32[1024,2048]{1,0:T(8,128)})) %all-reduce.99.cloned.1.call-update) | async-done | bytes 16777232 | tf_op jit(solution)/shard_map/psum | solution.py:182
  2604.9 39.3 %all-reduce.83 = (f32[2048]{0:T(1024)}, f32[4,640]{1,0:T(4,128)}, f32[640]{0:T(1024)}, f32[640]{0:T(1024)}, f32[640]{0:T(1024)}, /*index=5*/f32[640]{0:T(1024)}, f32[2048]{0:T(1024)}) all-reduce(f32[2048]{0:T(1024)S(1)} %get-tuple-element.283, ...), channel_id=1, replica_groups=mesh['fsdp'=4,'ctx'=2,'tp'=4] {'fsdp','ctx'}, use_global_device_ids=true, to_apply=%region_13.14 | all-reduce | flops 9216 | bytes 73728 | tf_op jit(solution)/shard_map/psum | solution.py:280
  2662.3 25.7 all-reduce.97.cloned.1.call-done
  2688.0 307.0 %all-reduce.101.cloned.1.call-done = (f32[512,640]{1,0:T(8,128)}, f32[512,640]{1,0:T(8,128)}, f32[640,512]{1,0:T(8,128)}, f32[512,1536]{1,0:T(8,128)}, f32[512,1536]{1,0:T(8,128)}, /*index=5*/f32[1536,512]{1,0:T(8,128)}) async-done(((f32[512,640]{1,0:T(8,128)}, f32[512,640]{1,0:T(8,128)}, f32[640,512]{1,0:T(8,128)}, f32[512,1536]{1,0:T(8,128)}, f32[512,1536]{1,0:T(8,128)}, ...) | async-done | bytes 13369360 | tf_op jit(solution)/shard_map/psum | solution.py:276
  (728 shorter events, 840.2 us)
Async XLA Ops:
  7.2 79.2 %copy-start = (bf16[4,160,160]{2,1,0:T(8,128)(2,1)S(1)}, bf16[4,160,160]{2,1,0:T(8,128)(2,1)}, u32[]{:S(2)}) copy-start(bf16[4,160,160]{2,1,0:T(8,128)(2,1)} %param.30) | copy-start | bytes 614404
  7.2 59.9 %all-gather.7.cloned.1.call-start = ((), (), s32[]{:S(2)}) async-start(), calls=%async_computation.6 | async-start | bytes 3276800 | tf_op jit(solution)/shard_map/all_gather | solution.py:90
  7.9 369.2 %all-gather.9.cloned.1.call-start = ((), (), s32[]{:S(2)}) async-start(), calls=%async_computation.7 | async-start | bytes 3276800 | tf_op jit(solution)/shard_map/all_gather | solution.py:89
  8.7 381.2 %all-gather.11.cloned.1.call-start = ((), (), s32[]{:S(2)}) async-start(), calls=%async_computation.8 | async-start | bytes 3276800 | tf_op jit(solution)/shard_map/all_gather | solution.py:93
  9.5 541.8 %all-reduce.93.cloned.1.call-start = ((), (), s32[]{:S(2)}) async-start(), calls=%async_computation.9 | async-start | bytes 16777216 | tf_op jit(solution)/shard_map/psum | solution.py:173
  12.7 65.6 %copy-start.76 = (f32[640]{0:T(1024)}, f32[640]{0:T(1024)S(1)}, u32[]{:S(2)}) copy-start(f32[640]{0:T(1024)S(1)} %get-tuple-element.290) | copy-start | bytes 7684
  12.7 65.6 %copy-start.78 = (f32[640]{0:T(1024)}, f32[640]{0:T(1024)S(1)}, u32[]{:S(2)}) copy-start(f32[640]{0:T(1024)S(1)} %get-tuple-element.291) | copy-start | bytes 7684
  12.7 81.2 %copy-start.60 = (f32[640]{0:T(1024)}, f32[640]{0:T(1024)S(1)}, u32[]{:S(2)}) copy-start(f32[640]{0:T(1024)S(1)} %fusion.106) | copy-start | bytes 7684
  73.6 4.7 collective-permute-start
  398.9 269.3 %all-gather.13.cloned.1.call-start = ((), (), s32[]{:S(2)}) async-start(), calls=%async_computation.10 | async-start | bytes 7864320 | tf_op jit(solution)/shard_map/all_gather | solution.py:91
  399.5 383.6 %all-gather.15.cloned.1.call-start = ((), (), s32[]{:S(2)}) async-start(), calls=%async_computation.11 | async-start | bytes 7864320 | tf_op jit(solution)/shard_map/all_gather | solution.py:92
  400.0 498.2 %all-gather.17.cloned.1.call-start = ((), (), s32[]{:S(2)}) async-start(), calls=%async_computation.12 | async-start | bytes 7864320 | tf_op jit(solution)/shard_map/all_gather | solution.py:94
  400.8 159.6 %copy-start.65 = (f32[2048]{0:T(1024)S(1)}, f32[2048]{0:T(1024)}, u32[]{:S(2)}) copy-start(f32[2048]{0:T(1024)} %param.36) | copy-start | bytes 24580
  400.8 687.6 %all-reduce.95.cloned.1.call-start = ((), (), s32[]{:S(2)}) async-start(), calls=%async_computation.13 | async-start | bytes 16777216 | tf_op jit(solution)/shard_map/psum | solution.py:192
  937.2 695.4 %reduce-scatter.11.cloned.1.call-start = ((), (), s32[]{:S(2)}) async-start(), calls=%async_computation.16 | async-start | bytes 6553600 | tf_op jit(solution)/shard_map/reduce_scatter | solution.py:272
  1110.4 522.2 %reduce-scatter.7.cloned.1.call-start = ((), (), s32[]{:S(2)}) async-start(), calls=%async_computation.14 | async-start | bytes 6553600 | tf_op jit(solution)/shard_map/reduce_scatter | solution.py:268
  1342.2 319.9 %reduce-scatter.9.cloned.1.call-start = ((), (), s32[]{:S(2)}) async-start(), calls=%async_computation.15 | async-start | bytes 6553600 | tf_op jit(solution)/shard_map/reduce_scatter | solution.py:269
  1554.1 5.6 collective-permute-start.1
  1568.8 307.9 %reduce-scatter.13.cloned.1.call-start = ((), (), s32[]{:S(2)}) async-start(), calls=%async_computation.17 | async-start | bytes 15728640 | tf_op jit(solution)/shard_map/reduce_scatter | solution.py:270
  1581.5 510.5 %reduce-scatter.15.cloned.1.call-start = ((), (), s32[]{:S(2)}) async-start(), calls=%async_computation.18 | async-start | bytes 15728640 | tf_op jit(solution)/shard_map/reduce_scatter | solution.py:271
  1594.1 713.1 %reduce-scatter.17.cloned.1.call-start = ((), (), s32[]{:S(2)}) async-start(), calls=%async_computation.19 | async-start | bytes 15728640 | tf_op jit(solution)/shard_map/reduce_scatter | solution.py:273
  1606.4 992.6 %all-reduce.99.cloned.1.call-start = ((), (), s32[]{:S(2)}) async-start(), calls=%async_computation.21 | async-start | bytes 33554432 | tf_op jit(solution)/shard_map/psum | solution.py:182
  1627.9 1060.1 %all-reduce.97.cloned.1.call-start = ((), (), s32[]{:S(2)}) async-start(), calls=%async_computation.20 | async-start | bytes 2621440 | tf_op jit(solution)/shard_map/psum | solution.py:280
  1632.5 1362.5 %all-reduce.101.cloned.1.call-start = ((), (), s32[]{:S(2)}) async-start(), calls=%async_computation.22 | async-start | bytes 26738688 | tf_op jit(solution)/shard_map/psum | solution.py:276
  (138 other events, 1560.3 us)
Sparse Core Ops, SparseCore 0:
  9.6 57.4 all-gather.6
  68.6 53.5 all-gather.8
  123.8 53.4 all-gather.10
  399.0 152.1 all-reduce.92
  552.6 115.4 all-gather.12
  669.6 113.5 all-gather.14
  784.7 113.5 all-gather.16
  937.3 151.0 all-reduce.94
  1110.5 93.9 reduce-scatter.10
  1342.3 93.8 reduce-scatter.6
  1568.9 93.1 reduce-scatter.8
  1664.3 212.3 reduce-scatter.12
  1879.1 212.8 reduce-scatter.14
  2094.2 212.8 reduce-scatter.16
  2309.7 289.3 all-reduce.98
  2603.6 84.3 all-reduce.96
  2690.8 304.0 all-reduce.100
where the time goes:
time: 3040 us; the launch traced here: 3020 us
  waiting for transfers between devices  1970 us (65%)
  local copies, waits for them, and re-layouts  565 us (19%)
  other arithmetic  203 us (7%)
  matrix products  194 us (6%)
  blocking collectives  56.9 us (2%)
    psum x1, waiting for transfers between devices, shards(): lax.psum((owned_branch, owned_input, owned_gate, owned_up, owned_out, own...  307 us
    psum x1, waiting for transfers between devices, shards(): output = (resid_rows + lax.psum(down_term, 'tp')).astype(jnp.bfloat16)  291 us
    reduce_scatter x1, waiting for transfers between devices, shards(): lax.psum_scatter(grad_w_up, 'fsdp', scatter_dimension=0, tiled=True)  215 us
    reduce_scatter x1, waiting for transfers between devices, shards(): lax.psum_scatter(grad_w_down, 'fsdp', scatter_dimension=1, tiled=True)  215 us
    reduce_scatter x1, waiting for transfers between devices, shards(): lax.psum_scatter(grad_w_gate, 'fsdp', scatter_dimension=0, tiled=True)  215 us
    slice x70, local copies, waits for them, and re-layouts, shards(): lax.associative_scan(linear_combine, (jnp.flip(next_factor, 1), jnp.flip(...  170 us
    psum x1, waiting for transfers between devices, shards(): grad_norm_mlp = lax.psum(mlp_back_term, 'tp')  151 us
    psum x1, waiting for transfers between devices, shards(): resid_rows = inputs + lax.psum(mixer_term, 'tp')  150 us
  transfers between devices with their start and end apart: 19, of which 15 were waited for; matrix products, arithmetic and copies ran while one was open for 29% of the time, Pallas kernels for 0%

commit v1 on v0

--- a/solution.py
+++ b/solution.py
@@ -5,6 +5,32 @@
 
 EPSILON = 1e-06
 RATE_SCALE = 8.0
+
+
+def goods_see(in_array, which_dim):
+    res = list(in_array.shape[1:])
+    res[which_dim] *= in_array.shape[0]
+    return jnp.moveaxis(in_array, 0, which_dim).reshape(res)
+
+
+def spot_guide(patch, row_axis, ndim_at):
+    axis_n = lax.axis_size(row_axis)
+    panels = tuple(((q, (q + 1) % axis_n) for q in range(axis_n)))
+    blocks_here = tuple(((nth, rr) for rr, nth in panels))
+    part_next, arr_out = ([], [])
+    for h in range(axis_n - 1):
+        if h % 2 == 0:
+            block_next = lax.ppermute(part_next[-1] if part_next else patch, row_axis, panels)
+            part_next.append(block_next)
+        else:
+            inter = lax.ppermute(arr_out[-1] if arr_out else patch, row_axis, blocks_here)
+            arr_out.append(inter)
+    z_new = jnp.stack([*part_next[::-1], patch, *arr_out], axis=0)
+    after = lax.axis_index(row_axis)
+    big = len(part_next)
+    found_now = after - big
+    z_new = z_new[(jnp.arange(axis_n) - found_now) % axis_n]
+    return goods_see(z_new, ndim_at)
 
 
 def passed_along(block, axis, distance):
@@ -91,7 +117,7 @@
         lax.all_gather(w_gate, "fsdp", axis=0, tiled=True),
         lax.all_gather(w_up, "fsdp", axis=0, tiled=True),
         lax.all_gather(w_out, "fsdp", axis=1, tiled=True),
-        lax.all_gather(w_down, "fsdp", axis=1, tiled=True),
+        spot_guide(w_down, "fsdp", 1),
     )
     seq_count, tok_count, model_width = tokens.shape
     row_count = seq_count * tok_count

time: 3040 us -> 2870 us (0.944)
  waiting for transfers between devices: 1970 us -> 1820 us
  starting transfers between devices: 5.35 us -> 36.9 us
    psum x1, waiting for transfers between devices: 150 us -> 28.2 us  [shards(): resid_rows = inputs + lax.psum(mixer_term, 'tp')]
    all_gather x1 -> x0, waiting for transfers between devices: 103 us -> none  [shards(): lax.all_gather(w_down, 'fsdp', axis=1, tiled=True)]
    ppermute x0 -> x3, waiting for transfers between devices: none -> 70.7 us  [the longest x2 68.3 us: spot_guide(): lax.ppermute(part_next[-1] if part_next else patch, row_axis, panels)]
    pad x36, local copies, waits for them, and re-layouts: 76.9 us -> 34.2 us  [shards(): lax.associative_scan(linear_combine, (carry_factor, driven), axis=1)]
    ppermute x0 -> x3, starting transfers between devices: none -> 31.6 us  [the longest x2 27.7 us: spot_guide(): lax.ppermute(part_next[-1] if part_next else patch, row_axis, panels)]
  transfers between devices with their start and end apart: 19 -> 21, of which waited for: 15 -> 17; matrix products, arithmetic and copies ran while one was open for 29% -> 29% of each run, Pallas kernels for 0% -> 0%
where the time goes in v1:
time: 2870 us; the launch traced here: 2850 us
  waiting for transfers between devices  1820 us (63%)
  local copies, waits for them, and re-layouts  540 us (19%)
  other arithmetic  191 us (7%)
  matrix products  190 us (7%)
  blocking collectives  56.9 us (2%)
  starting transfers between devices  36.9 us (1%)
    psum x1, waiting for transfers between devices, shards(): lax.psum((owned_branch, owned_input, owned_gate, owned_up, owned_out, own...  307 us
    psum x1, waiting for transfers between devices, shards(): output = (resid_rows + lax.psum(down_term, 'tp')).astype(jnp.bfloat16)  291 us
    reduce_scatter x1, waiting for transfers between devices, shards(): lax.psum_scatter(grad_w_down, 'fsdp', scatter_dimension=1, tiled=True)  215 us
    reduce_scatter x1, waiting for transfers between devices, shards(): lax.psum_scatter(grad_w_up, 'fsdp', scatter_dimension=0, tiled=True)  215 us
    reduce_scatter x1, waiting for transfers between devices, shards(): lax.psum_scatter(grad_w_gate, 'fsdp', scatter_dimension=0, tiled=True)  215 us
    slice x70, local copies, waits for them, and re-layouts, shards(): lax.associative_scan(linear_combine, (jnp.flip(next_factor, 1), jnp.flip(...  171 us
    psum x1, waiting for transfers between devices, shards(): grad_norm_mlp = lax.psum(mlp_back_term, 'tp')  151 us
    slice x68, local copies, waits for them, and re-layouts, shards(): lax.associative_scan(linear_combine, (carry_factor, driven), axis=1)  130 us
  transfers between devices with their start and end apart: 21, of which 17 were waited for; matrix products, arithmetic and copies ran while one was open for 29% of the time, Pallas kernels for 0%

profile of v1, /device:TPU:0, one launch (start us, length us, event | category | flops | bytes accessed | tf_op | source)
XLA Modules:
  0.0 2849.6 jit_solution(7622508120511195051)
XLA Ops:
  13.5 53.5 %all-gather.6.cloned.1.call-done = bf16[2048,640]{1,0:T(8,128)(2,1)} async-done(((bf16[512,640]{1,0:T(8,128)(2,1)}), bf16[2048,640]{1,0:T(8,128)(2,1)}) %all-gather.6.cloned.1.call-update) | async-done | bytes 2621456 | tf_op jit(solution)/shard_map/all_gather | solution.py:116
  316.4 12.4 fusion.77
  341.9 35.2 %collective-permute-done.1 = bf16[1536,512]{1,0:T(8,128)(2,1)S(1)} collective-permute-done((bf16[1536,512]{1,0:T(8,128)(2,1)S(1)}, bf16[1536,512]{1,0:T(8,128)(2,1)S(1)}, u32[]{:S(2)}, u32[]{:S(2)}) %collective-permute-start.1) | collective-permute-done | bytes 1572896 | tf_op jit(solution)/shard_map/ppermute | solution.py:23
  377.1 27.7 collective-permute-start.2
  407.3 33.0 %collective-permute-done.2 = bf16[1536,512]{1,0:T(8,128)(2,1)} collective-permute-done((bf16[1536,512]{1,0:T(8,128)(2,1)S(1)}, bf16[1536,512]{1,0:T(8,128)(2,1)}, u32[]{:S(2)}, u32[]{:S(2)}) %collective-permute-start.2) | collective-permute-done | bytes 1572896 | tf_op jit(solution)/shard_map/ppermute | solution.py:23
  460.8 28.2 all-reduce.93.cloned.1.call-done
  500.9 105.0 %all-gather.12.cloned.1.call-done = bf16[2048,1536]{1,0:T(8,128)(2,1)} async-done(((bf16[512,1536]{1,0:T(8,128)(2,1)}), bf16[2048,1536]{1,0:T(8,128)(2,1)}) %all-gather.12.cloned.1.call-update) | async-done | bytes 6291472 | tf_op jit(solution)/shard_map/all_gather | solution.py:117
  617.7 103.3 %all-gather.14.cloned.1.call-done = bf16[2048,1536]{1,0:T(8,128)(2,1)} async-done(((bf16[512,1536]{1,0:T(8,128)(2,1)}), bf16[2048,1536]{1,0:T(8,128)(2,1)}) %all-gather.14.cloned.1.call-update) | async-done | bytes 6291472 | tf_op jit(solution)/shard_map/all_gather | solution.py:118
  732.8 15.8 fusion.25
  769.0 151.1 %all-reduce.95.cloned.1.call-done = f32[1024,2048]{1,0:T(8,128)} async-done(((f32[1024,2048]{1,0:T(8,128)}), f32[1024,2048]{1,0:T(8,128)}) %all-reduce.95.cloned.1.call-update) | async-done | bytes 8388624 | tf_op jit(solution)/shard_map/psum | solution.py:218
  999.8 12.3 fusion.55
  1012.1 20.8 reverse.9
  1311.6 20.8 rev.13
  1332.4 21.0 rev.12
  1402.3 12.9 fusion.148
  1415.3 12.5 fusion.149
  1466.3 29.3 %reduce-scatter.9.cloned.1.call-done = f32[512,640]{1,0:T(8,128)} async-done(((f32[2048,640]{1,0:T(8,128)}), f32[512,640]{1,0:T(8,128)}) %reduce-scatter.9.cloned.1.call-update) | async-done | bytes 1310736 | tf_op jit(solution)/shard_map/reduce_scatter | solution.py:295
  1495.6 214.8 %reduce-scatter.13.cloned.1.call-done = f32[512,1536]{1,0:T(8,128)} async-done(((f32[2048,1536]{1,0:T(8,128)}), f32[512,1536]{1,0:T(8,128)}) %reduce-scatter.13.cloned.1.call-update) | async-done | bytes 3145744 | tf_op jit(solution)/shard_map/reduce_scatter | solution.py:296
  1710.4 215.2 %reduce-scatter.15.cloned.1.call-done = f32[512,1536]{1,0:T(8,128)} async-done(((f32[2048,1536]{1,0:T(8,128)}), f32[512,1536]{1,0:T(8,128)}) %reduce-scatter.15.cloned.1.call-update) | async-done | bytes 3145744 | tf_op jit(solution)/shard_map/reduce_scatter | solution.py:297
  1925.6 215.3 %reduce-scatter.17.cloned.1.call-done = f32[1536,512]{1,0:T(8,128)} async-done(((f32[1536,2048]{1,0:T(8,128)}), f32[1536,512]{1,0:T(8,128)}) %reduce-scatter.17.cloned.1.call-update) | async-done | bytes 3145744 | tf_op jit(solution)/shard_map/reduce_scatter | solution.py:299
  2141.6 291.2 %all-reduce.99.cloned.1.call-done = (f32[1024,2048]{1,0:T(8,128)}, f32[1024,2048]{1,0:T(8,128)}) async-done(((f32[1024,2048]{1,0:T(8,128)}, f32[1024,2048]{1,0:T(8,128)}), (f32[1024,2048]{1,0:T(8,128)}, f32[1024,2048]{1,0:T(8,128)})) %all-reduce.99.cloned.1.call-update) | async-done | bytes 16777232 | tf_op jit(solution)/shard_map/psum | solution.py:208
  2438.6 39.3 %all-reduce.83 = (f32[2048]{0:T(1024)}, f32[4,640]{1,0:T(4,128)}, f32[640]{0:T(1024)}, f32[640]{0:T(1024)}, f32[640]{0:T(1024)}, /*index=5*/f32[640]{0:T(1024)}, f32[2048]{0:T(1024)}) all-reduce(f32[2048]{0:T(1024)S(1)} %get-tuple-element.283, ...), channel_id=1, replica_groups=mesh['fsdp'=4,'ctx'=2,'tp'=4] {'fsdp','ctx'}, use_global_device_ids=true, to_apply=%region_13.14 | all-reduce | flops 9216 | bytes 73728 | tf_op jit(solution)/shard_map/psum | solution.py:306
  2496.0 25.7 all-reduce.97.cloned.1.call-done
  2521.7 307.0 %all-reduce.101.cloned.1.call-done = (f32[512,640]{1,0:T(8,128)}, f32[512,640]{1,0:T(8,128)}, f32[640,512]{1,0:T(8,128)}, f32[512,1536]{1,0:T(8,128)}, f32[512,1536]{1,0:T(8,128)}, /*index=5*/f32[1536,512]{1,0:T(8,128)}) async-done(((f32[512,640]{1,0:T(8,128)}, f32[512,640]{1,0:T(8,128)}, f32[640,512]{1,0:T(8,128)}, f32[512,1536]{1,0:T(8,128)}, f32[512,1536]{1,0:T(8,128)}, ...) | async-done | bytes 13369360 | tf_op jit(solution)/shard_map/psum | solution.py:302
  (725 shorter events, 830.0 us)
Async XLA Ops:
  7.2 79.0 %copy-start = (bf16[4,160,160]{2,1,0:T(8,128)(2,1)S(1)}, bf16[4,160,160]{2,1,0:T(8,128)(2,1)}, u32[]{:S(2)}) copy-start(bf16[4,160,160]{2,1,0:T(8,128)(2,1)} %param.30) | copy-start | bytes 614404
  7.2 59.9 %all-gather.6.cloned.1.call-start = ((), (), s32[]{:S(2)}) async-start(), calls=%async_computation.6 | async-start | bytes 3276800 | tf_op jit(solution)/shard_map/all_gather | solution.py:116
  7.9 308.4 %all-gather.8.cloned.1.call-start = ((), (), s32[]{:S(2)}) async-start(), calls=%async_computation.7 | async-start | bytes 3276800 | tf_op jit(solution)/shard_map/all_gather | solution.py:115
  8.7 320.1 %all-gather.10.cloned.1.call-start = ((), (), s32[]{:S(2)}) async-start(), calls=%async_computation.8 | async-start | bytes 3276800 | tf_op jit(solution)/shard_map/all_gather | solution.py:119
  9.5 479.6 %all-reduce.93.cloned.1.call-start = ((), (), s32[]{:S(2)}) async-start(), calls=%async_computation.9 | async-start | bytes 16777216 | tf_op jit(solution)/shard_map/psum | solution.py:199
  12.7 65.6 %copy-start.73 = (f32[640]{0:T(1024)}, f32[640]{0:T(1024)S(1)}, u32[]{:S(2)}) copy-start(f32[640]{0:T(1024)S(1)} %get-tuple-element.290) | copy-start | bytes 7684
  12.7 81.1 %copy-start.61 = (f32[640]{0:T(1024)}, f32[640]{0:T(1024)S(1)}, u32[]{:S(2)}) copy-start(f32[640]{0:T(1024)S(1)} %fusion.107) | copy-start | bytes 7684
  73.6 4.7 collective-permute-start
  336.7 269.3 %all-gather.12.cloned.1.call-start = ((), (), s32[]{:S(2)}) async-start(), calls=%async_computation.10 | async-start | bytes 7864320 | tf_op jit(solution)/shard_map/all_gather | solution.py:117
  337.3 383.7 %all-gather.14.cloned.1.call-start = ((), (), s32[]{:S(2)}) async-start(), calls=%async_computation.11 | async-start | bytes 7864320 | tf_op jit(solution)/shard_map/all_gather | solution.py:118
  337.8 582.3 %all-reduce.95.cloned.1.call-start = ((), (), s32[]{:S(2)}) async-start(), calls=%async_computation.12 | async-start | bytes 16777216 | tf_op jit(solution)/shard_map/psum | solution.py:218
  338.1 39.1 %collective-permute-start.1 = (bf16[1536,512]{1,0:T(8,128)(2,1)S(1)}, bf16[1536,512]{1,0:T(8,128)(2,1)S(1)}, u32[]{:S(2)}, u32[]{:S(2)}) collective-permute-start(bf16[1536,512]{1,0:T(8,128)(2,1)S(1)} %copy-done.42), channel_id=1, source_target_pairs={{0,8},{8,16},{16,24},{24,0},{1,9},{9,17},{17,25},{25,1},{2,10},{10... | collective-permute-start | bytes 4718600 | tf_op jit(solution)/shard_map/ppermute | solution.py:23
  338.1 69.2 %collective-permute-start.3 = (bf16[1536,512]{1,0:T(8,128)(2,1)S(1)}, bf16[1536,512]{1,0:T(8,128)(2,1)}, u32[]{:S(2)}, u32[]{:S(2)}) collective-permute-start(bf16[1536,512]{1,0:T(8,128)(2,1)S(1)} %copy-done.42), channel_id=1, source_target_pairs={{8,0},{16,8},{24,16},{0,24},{9,1},{17,9},{25,17},{1,25},{10,2},{18... | collective-permute-start | bytes 4718600 | tf_op jit(solution)/shard_map/ppermute | solution.py:26
  377.1 63.2 %collective-permute-start.2 = (bf16[1536,512]{1,0:T(8,128)(2,1)S(1)}, bf16[1536,512]{1,0:T(8,128)(2,1)}, u32[]{:S(2)}, u32[]{:S(2)}) collective-permute-start(bf16[1536,512]{1,0:T(8,128)(2,1)S(1)} %collective-permute-done.1), channel_id=1, source_target_pairs={{0,8},{8,16},{16,24},{24,0},{1,9},{9,17},{17,25},{25,1},{2,10},{10... | collective-permute-start | bytes 4718600 | tf_op jit(solution)/shard_map/ppermute | solution.py:23
  768.9 697.3 %reduce-scatter.11.cloned.1.call-start = ((), (), s32[]{:S(2)}) async-start(), calls=%async_computation.15 | async-start | bytes 6553600 | tf_op jit(solution)/shard_map/reduce_scatter | solution.py:298
  942.1 524.2 %reduce-scatter.7.cloned.1.call-start = ((), (), s32[]{:S(2)}) async-start(), calls=%async_computation.13 | async-start | bytes 6553600 | tf_op jit(solution)/shard_map/reduce_scatter | solution.py:294
  1175.9 319.7 %reduce-scatter.9.cloned.1.call-start = ((), (), s32[]{:S(2)}) async-start(), calls=%async_computation.14 | async-start | bytes 6553600 | tf_op jit(solution)/shard_map/reduce_scatter | solution.py:295
  1387.5 5.6 collective-permute-start.4
  1402.2 308.2 %reduce-scatter.13.cloned.1.call-start = ((), (), s32[]{:S(2)}) async-start(), calls=%async_computation.16 | async-start | bytes 15728640 | tf_op jit(solution)/shard_map/reduce_scatter | solution.py:296
  1415.2 510.4 %reduce-scatter.15.cloned.1.call-start = ((), (), s32[]{:S(2)}) async-start(), calls=%async_computation.17 | async-start | bytes 15728640 | tf_op jit(solution)/shard_map/reduce_scatter | solution.py:297
  1427.8 713.1 %reduce-scatter.17.cloned.1.call-start = ((), (), s32[]{:S(2)}) async-start(), calls=%async_computation.18 | async-start | bytes 15728640 | tf_op jit(solution)/shard_map/reduce_scatter | solution.py:299
  1440.1 992.6 %all-reduce.99.cloned.1.call-start = ((), (), s32[]{:S(2)}) async-start(), calls=%async_computation.20 | async-start | bytes 33554432 | tf_op jit(solution)/shard_map/psum | solution.py:208
  1461.6 1060.1 %all-reduce.97.cloned.1.call-start = ((), (), s32[]{:S(2)}) async-start(), calls=%async_computation.19 | async-start | bytes 2621440 | tf_op jit(solution)/shard_map/psum | solution.py:306
  1466.2 1362.5 %all-reduce.101.cloned.1.call-start = ((), (), s32[]{:S(2)}) async-start(), calls=%async_computation.21 | async-start | bytes 26738688 | tf_op jit(solution)/shard_map/psum | solution.py:302
  (134 other events, 1504.3 us)
Sparse Core Ops, SparseCore 0:
  9.6 57.4 all-gather.5
  68.6 53.5 all-gather.7
  123.8 53.4 all-gather.9
  336.8 152.2 all-reduce.92
  490.5 115.4 all-gather.11
  607.4 113.5 all-gather.13
  769.1 151.0 all-reduce.94
  942.2 93.9 reduce-scatter.10
  1176.0 93.9 reduce-scatter.6
  1402.4 93.2 reduce-scatter.8
  1498.0 212.3 reduce-scatter.12
  1712.6 212.8 reduce-scatter.14
  1927.9 212.8 reduce-scatter.16
  2143.4 289.3 all-reduce.98
  2437.4 84.3 all-reduce.96
  2524.6 304.0 all-reduce.100
